TPU v7x, 32 devices: a whole 2x2x4 slice. The times are simulated.
32 devices in a mesh: dp: 8 (over z, y), expert: 4 (over x, core).
Axes of the slice: x: 2, y: 2, z: 4, core: 2. Of those that a mesh axis runs over, the one named last changes fastest.
Arguments:
- tokens: bfloat16 [4096, 2048], P(('dp', 'expert')), may hold values from -6 to 6
- routes: int32 [4096, 8], P(('dp', 'expert')), may hold values from 0 to 15, all different within a row; in each aligned block of 128 rows (0 to 127, 128 to 255, ...) at most 80 rows name the same one
- gates: bfloat16 [4096, 8], P(('dp', 'expert')), may hold values from 0.099609375 to 0.5
- cotangent: bfloat16 [4096, 2048], P(('dp', 'expert')), may hold values from -6 to 6
- w_gate: bfloat16 [16, 2048, 384], P('dp'), may hold values from -0.125 to 0.125
- w_up: bfloat16 [16, 2048, 384], P('dp'), may hold values from -0.125 to 0.125
- w_down: bfloat16 [16, 384, 2048], P('dp'), may hold values from -0.3125 to 0.3125
Outputs:
- layer_out: bfloat16 [4096, 2048], P(('dp', 'expert'))
- grad_tokens: bfloat16 [4096, 2048], P(('dp', 'expert'))
- grad_gate: bfloat16 [16, 2048, 384], P('dp', 'expert')
- grad_up: bfloat16 [16, 2048, 384], P('dp', 'expert')
- grad_down: bfloat16 [16, 384, 2048], P('dp', None, 'expert')
Inputs may be any that keep to these rules, and one draw needn't show every extreme that they name: `routes`: each row names 8 different experts. Among the rows of one device, no expert is named by more than 80 rows, and in every draw some device has an expert named by exactly 80 rows.
All inputs are finite; a program needn't handle non-finite values.
Results may differ from a plain program's by a relative error of at most 0.012.
Values may be sent and summed in bfloat16 or wider, within the bound.
A program may use at most 128 MiB of HBM per device.

v0:
```python
import jax
import jax.numpy as jnp
from jax import lax
from jax.sharding import PartitionSpec as P


def expert_forward(arrived, w_gate, w_up, w_down):
    gate_act = jnp.einsum("erd,edf->erf", arrived, w_gate, preferred_element_type=jnp.float32)
    up_act = jnp.einsum("erd,edf->erf", arrived, w_up, preferred_element_type=jnp.float32)
    sigma_gate = jax.nn.sigmoid(gate_act)
    smooth = gate_act * sigma_gate
    hidden = (smooth * up_act).astype(jnp.bfloat16)
    result = jnp.einsum("erf,efd->erd", hidden, w_down, preferred_element_type=jnp.float32).astype(
        jnp.bfloat16
    )
    return (gate_act, up_act, sigma_gate, smooth, hidden, result)


def body(tokens, routes, gates, cotangent, w_gate, w_up, w_down):
    tok_rows, top_k = routes.shape
    width = tokens.shape[1]
    owners = lax.axis_size("dp")
    per_owner = w_gate.shape[0]
    hidden_units = w_gate.shape[2]
    experts = owners * per_owner
    capacity = max(2, tok_rows * top_k * 5 // (4 * experts))
    slot_count = experts * capacity
    chosen = routes.reshape(-1)
    onehot = (chosen[:, None] == jnp.arange(experts, dtype=jnp.int32)[None, :]).astype(jnp.int32)
    order_in = jnp.sum((jnp.cumsum(onehot, axis=0) - onehot) * onehot, axis=1)
    slot_index = chosen * capacity + order_in
    token_of = jnp.arange(tok_rows * top_k, dtype=jnp.int32) // top_k
    table = jnp.full((slot_count,), tok_rows, jnp.int32).at[slot_index].set(token_of)
    slot_gain = (
        jnp.zeros((slot_count,), jnp.float32)
        .at[slot_index]
        .set(gates.reshape(-1).astype(jnp.float32))
    )
    padded_x = jnp.concatenate([tokens, jnp.zeros((1, width), tokens.dtype)], axis=0)
    padded_c = jnp.concatenate([cotangent, jnp.zeros((1, width), cotangent.dtype)], axis=0)
    send_rows = padded_x[table].reshape(experts, capacity, width)
    send_grads = (slot_gain[:, None] * padded_c[table].astype(jnp.float32)).astype(jnp.bfloat16)
    send_grads = send_grads.reshape(experts, capacity, width)
    arrived = lax.all_to_all(send_rows, "dp", split_axis=0, concat_axis=1, tiled=True)
    state = expert_forward(arrived, w_gate, w_up, w_down)
    arrived_grad = lax.all_to_all(send_grads, "dp", split_axis=0, concat_axis=1, tiled=True)
    gate_act, up_act, sigma_gate, smooth, hidden, result = state
    returned = lax.all_to_all(result, "dp", split_axis=1, concat_axis=0, tiled=True).reshape(
        slot_count, width
    )
    picked = returned[slot_index].reshape(tok_rows, top_k, width)
    layer_out = jnp.einsum("tk,tkd->td", gates, picked, preferred_element_type=jnp.float32).astype(
        jnp.bfloat16
    )
    grad_hidden = jnp.einsum(
        "erd,efd->erf", arrived_grad, w_down, preferred_element_type=jnp.float32
    )
    grad_upact = (grad_hidden * smooth).astype(jnp.bfloat16)
    grad_gateact = (
        grad_hidden * up_act * sigma_gate * (1.0 + gate_act * (1.0 - sigma_gate))
    ).astype(jnp.bfloat16)
    row_grads = (
        jnp.einsum("erf,edf->erd", grad_gateact, w_gate, preferred_element_type=jnp.float32)
        + jnp.einsum("erf,edf->erd", grad_upact, w_up, preferred_element_type=jnp.float32)
    ).astype(jnp.bfloat16)
    came_back = lax.all_to_all(row_grads, "dp", split_axis=1, concat_axis=0, tiled=True).reshape(
        slot_count, width
    )
    grad_picked = came_back[slot_index].reshape(tok_rows, top_k, width)
    grad_tokens = jnp.sum(grad_picked.astype(jnp.float32), axis=1).astype(jnp.bfloat16)
    both_factors = jnp.concatenate([grad_gateact, grad_upact], axis=2)
    input_term = jnp.einsum(
        "erd,erf->def", arrived, both_factors, preferred_element_type=jnp.float32
    )
    down_term = jnp.einsum("erf,erd->def", hidden, arrived_grad, preferred_element_type=jnp.float32)
    totals = lax.psum_scatter(
        jnp.concatenate([input_term, down_term], axis=2).astype(jnp.bfloat16),
        "expert",
        scatter_dimension=0,
        tiled=True,
    ).astype(jnp.float32)
    grad_gate = jnp.transpose(totals[:, :, :hidden_units], (1, 0, 2)).astype(jnp.bfloat16)
    grad_up = jnp.transpose(totals[:, :, hidden_units : 2 * hidden_units], (1, 0, 2)).astype(
        jnp.bfloat16
    )
    grad_down = jnp.transpose(totals[:, :, 2 * hidden_units :], (1, 2, 0)).astype(jnp.bfloat16)
    return (layer_out, grad_tokens, grad_gate, grad_up, grad_down)


def solution(mesh):
    return jax.shard_map(
        body,
        mesh=mesh,
        in_specs=(
            P(("dp", "expert"), None),
            P(("dp", "expert"), None),
            P(("dp", "expert"), None),
            P(("dp", "expert"), None),
            P("dp", None, None),
            P("dp", None, None),
            P("dp", None, None),
        ),
        out_specs=(
            P(("dp", "expert"), None),
            P(("dp", "expert"), None),
            P("dp", "expert", None),
            P("dp", "expert", None),
            P("dp", None, "expert"),
        ),
        check_vma=False,
    )
```

profile of v0, /device:TPU:0, one launch (start us, length us, event | category | flops | bytes accessed | tf_op | source)
XLA Modules:
  0.0 627.4 jit_solution(449941669003016595)
XLA Ops:
  9.0 4.5 reduce-window.6
  14.2 4.3 scatter_custom_fusion
  19.4 4.3 scatter_custom_fusion.1
  25.7 11.9 %gather_fusion.2 = bf16[1280,2048]{1,0:T(8,128)(2,1)} fusion(bf16[129,2048]{1,0:T(8,128)(2,1)} %concatenate.14, s32[2048]{0:T(1024)S(1)} %pad_clamp_fusion), kind=kCustom, calls=%fused_computation.2 | custom fusion | bytes 10490880 | tf_op jit(solution)/shard_map/gather | solution.py:42
  37.7 5.7 fusion
  43.4 7.3 %all-to-all-start.2 = ((bf16[16,80,2048]{2,1,0:T(8,128)(2,1)}), bf16[16,80,2048]{2,1,0:T(8,128)(2,1)}, u32[]{:S(2)}, u32[]{:S(2)}) async-start(bf16[16,80,2048]{2,1,0:T(8,128)(2,1)} %fusion), calls=%async_computation.2 | async-start | bytes 10485760 | tf_op jit(solution)/shard_map/all_to_all | solution.py:46
  52.6 12.0 %gather_fusion = bf16[1280,2048]{1,0:T(8,128)(2,1)} fusion(bf16[129,2048]{1,0:T(8,128)(2,1)} %concatenate.13, s32[2048]{0:T(1024)S(1)} %pad_clamp_fusion), kind=kCustom, calls=%fused_computation | custom fusion | bytes 10490880 | tf_op jit(solution)/shard_map/gather | solution.py:41
  64.5 101.9 %all-to-all-done.2 = bf16[16,80,2048]{2,1,0:T(8,128)(2,1)} async-done(((bf16[16,80,2048]{2,1,0:T(8,128)(2,1)}), bf16[16,80,2048]{2,1,0:T(8,128)(2,1)}, u32[]{:S(2)}, u32[]{:S(2)}) %all-to-all-start.2) | async-done | bytes 5242912 | tf_op jit(solution)/shard_map/all_to_all | solution.py:46
  166.4 4.8 all-to-all-start
  171.3 5.6 copy.52
  176.9 109.3 %all-to-all-done = bf16[16,80,2048]{2,1,0:T(8,128)(2,1)} async-done(((bf16[16,80,2048]{2,1,0:T(8,128)(2,1)}), bf16[16,80,2048]{2,1,0:T(8,128)(2,1)}, u32[]{:S(2)}, u32[]{:S(2)}) %all-to-all-start) | async-done | bytes 5242912 | tf_op jit(solution)/shard_map/all_to_all | solution.py:44
  289.6 4.2 fusion.20
  293.8 4.1 fusion.21
  297.9 6.0 multiply_convert_fusion
  303.9 3.1 fusion.22
  307.1 7.1 %convert_bitcast_fusion = bf16[2048,2,768]{0,2,1:T(8,128)(2,1)} fusion(bf16[2,640,2048]{2,1,0:T(8,128)(2,1)S(1)} %bitcast.86, bf16[2,640,384]{1,2,0:T(8,128)(2,1)S(1)} %copy-done.7, bf16[2,640,384]{1,2,0:T(8,128)(2,1)S(1)} %get-tuple-element.21), kind=kOutput, calls=%fused_computation.10 | convolution fusion | flops 4033609728 | bytes 13500416 | tf_op jit(solution)/shard_map/erd,erf->def/dot_general | solution.py:72
  314.3 4.0 fusion.3
  318.2 5.2 add_convert_fusion
  323.4 10.2 %copy.55 = bf16[2,640,2048]{2,0,1:T(2,128)(2,1)} copy(bf16[2,640,2048]{2,1,0:T(8,128)(2,1)} %add_convert_fusion) | data formatting | bytes 10485760 | tf_op jit(solution)/shard_map/convert_element_type | solution.py:65
  333.6 4.7 all-to-all-start.3
  338.4 8.2 %pad_maximum_fusion = bf16[2048,2,1152]{0,2,1:T(8,128)(2,1)} fusion(bf16[2048,2,384]{0,2,1:T(8,128)(2,1)} %fusion.3, bf16[2048,2,768]{0,2,1:T(8,128)(2,1)} %convert_bitcast_fusion), kind=kLoop, calls=%fused_computation.9 | loop fusion | flops 18874368 | bytes 18874368 | tf_op jit(solution)/shard_map/concatenate | solution.py:77
  346.6 5.9 convolution_convert_fusion
  352.6 11.0 %copy.49 = bf16[2,640,2048]{2,0,1:T(2,128)(2,1)} copy(bf16[2,640,2048]{2,1,0:T(8,128)(2,1)} %convolution_convert_fusion) | data formatting | bytes 10485760 | tf_op jit(solution)/shard_map/convert_element_type | solution.py:13
  363.6 89.6 %all-to-all-done.3 = bf16[2,640,2048]{2,0,1:T(2,128)(2,1)} async-done(((bf16[2,640,2048]{2,0,1:T(2,128)(2,1)}), bf16[2,640,2048]{2,0,1:T(2,128)(2,1)}, u32[]{:S(2)}, u32[]{:S(2)}) %all-to-all-start.3) | async-done | bytes 5242912 | tf_op jit(solution)/shard_map/all_to_all | solution.py:66
  453.2 4.8 all-to-all-start.1
  458.2 7.2 %copy.56 = bf16[2,8,80,2048]{3,2,0,1:T(8,128)(2,1)} copy(bf16[2,8,80,2048]{3,0,2,1:T(2,128)(2,1)} %bitcast.18) | data formatting | bytes 10485760 | tf_op jit(solution)/shard_map/all_to_all | solution.py:66
  465.4 107.5 %all-to-all-done.1 = bf16[2,640,2048]{2,0,1:T(2,128)(2,1)} async-done(((bf16[2,640,2048]{2,0,1:T(2,128)(2,1)}), bf16[2,640,2048]{2,0,1:T(2,128)(2,1)}, u32[]{:S(2)}, u32[]{:S(2)}) %all-to-all-start.1) | async-done | bytes 5242912 | tf_op jit(solution)/shard_map/all_to_all | solution.py:48
  572.9 7.3 %copy.50 = bf16[2,8,80,2048]{3,2,0,1:T(8,128)(2,1)} copy(bf16[2,8,80,2048]{3,0,2,1:T(2,128)(2,1)} %bitcast.8) | data formatting | bytes 10485760 | tf_op jit(solution)/shard_map/all_to_all | solution.py:48
  580.2 12.0 %gather_fusion.3 = bf16[1024,2048]{1,0:T(8,128)(2,1)} fusion(bf16[1280,2048]{1,0:T(8,128)(2,1)} %bitcast.74, s32[1024]{0:T(1024)S(1)} %broadcast_clamp_fusion), kind=kCustom, calls=%fused_computation.3 | custom fusion | bytes 8392704 | tf_op jit(solution)/shard_map/gather | solution.py:69
  592.2 12.2 %gather_fusion.1 = bf16[1024,2048]{1,0:T(8,128)(2,1)} fusion(bf16[1280,2048]{1,0:T(8,128)(2,1)} %bitcast.75, s32[1024]{0:T(1024)S(1)} %broadcast_clamp_fusion), kind=kCustom, calls=%fused_computation.1 | custom fusion | bytes 8392704 | tf_op jit(solution)/shard_map/gather | solution.py:51
  604.3 3.6 fusion.1
  609.0 3.7 bitcast_reduce_fusion
  (65 shorter events, 19.6 us)
Async XLA Ops:
  7.2 290.7 %copy-start = (bf16[2,384,2048]{2,1,0:T(8,128)(2,1)S(1)}, bf16[2,384,2048]{2,1,0:T(8,128)(2,1)}, u32[]{:S(2)}) copy-start(bf16[2,384,2048]{2,1,0:T(8,128)(2,1)} %param.13) | copy-start | bytes 9437188
  43.4 123.1 %all-to-all-start.2 = ((bf16[16,80,2048]{2,1,0:T(8,128)(2,1)}), bf16[16,80,2048]{2,1,0:T(8,128)(2,1)}, u32[]{:S(2)}, u32[]{:S(2)}) async-start(bf16[16,80,2048]{2,1,0:T(8,128)(2,1)} %fusion), calls=%async_computation.2 | async-start | bytes 10485760 | tf_op jit(solution)/shard_map/all_to_all | solution.py:46
  166.4 119.7 %all-to-all-start = ((bf16[16,80,2048]{2,1,0:T(8,128)(2,1)}), bf16[16,80,2048]{2,1,0:T(8,128)(2,1)}, u32[]{:S(2)}, u32[]{:S(2)}) async-start(bf16[16,80,2048]{2,1,0:T(8,128)(2,1)} %bitcast.76), calls=%async_computation | async-start | bytes 10485760 | tf_op jit(solution)/shard_map/all_to_all | solution.py:44
  286.2 3.4 copy-start.4
  289.3 4.5 copy-start.2
  289.6 4.2 copy-start.5
  289.6 8.3 %slice-start = ((s8[5242880]{0:T(1024)(128)(4,1)}), s8[4194304]{0:T(1024)(128)(4,1)S(1)}, s32[]{:S(2)}) async-start(s8[5242880]{0:T(1024)(128)(4,1)} %bitcast.78), calls=%async_computation.6 | async-start | bytes 8388608
  293.8 4.1 slice-start.1
  303.9 3.2 copy-start.3
  303.9 3.2 copy-start.7
  303.9 10.3 %slice-start.2 = ((s8[5242880]{0:T(1024)(128)(4,1)}), s8[4194304]{0:T(1024)(128)(4,1)S(1)}, s32[]{:S(2)}) async-start(s8[5242880]{0:T(1024)(128)(4,1)} %bitcast.81), calls=%async_computation.8 | async-start | bytes 8388608
  307.1 7.2 %slice-start.3 = ((s8[5242880]{0:T(1024)(128)(4,1)}), s8[1048576]{0:T(1024)(128)(4,1)S(1)}, s32[]{:S(2)}) async-start(s8[5242880]{0:T(1024)(128)(4,1)} %bitcast.81), calls=%async_computation.9 | async-start | bytes 2097152
  307.1 7.1 %copy-start.10 = (bf16[2,640,384]{1,2,0:T(8,128)(2,1)S(1)}, bf16[2,640,384]{1,2,0:T(8,128)(2,1)}, u32[]{:S(2)}) copy-start(bf16[2,640,384]{1,2,0:T(8,128)(2,1)} %get-tuple-element.22) | copy-start | bytes 2949124
  314.2 4.0 copy-start.6
  314.2 4.0 copy-start.8
  333.6 119.6 %all-to-all-start.3 = ((bf16[2,640,2048]{2,0,1:T(2,128)(2,1)}), bf16[2,640,2048]{2,0,1:T(2,128)(2,1)}, u32[]{:S(2)}, u32[]{:S(2)}) async-start(bf16[2,640,2048]{2,0,1:T(2,128)(2,1)} %copy.55), calls=%async_computation.3 | async-start | bytes 10485760 | tf_op jit(solution)/shard_map/all_to_all | solution.py:66
  338.4 274.3 %reduce-scatter.2.cloned.1.call-start = ((), (), s32[]{:S(2)}) async-start(), calls=%async_computation.5 | async-start | bytes 11796480 | tf_op jit(solution)/shard_map/reduce_scatter | solution.py:76
  363.6 94.4 %copy-start.9 = (bf16[128,8]{0,1:T(8,128)(2,1)S(1)}, bf16[128,8]{0,1:T(8,128)(2,1)}, u32[]{:S(2)}) copy-start(bf16[128,8]{0,1:T(8,128)(2,1)} %param.9) | copy-start | bytes 6148
  453.2 119.7 %all-to-all-start.1 = ((bf16[2,640,2048]{2,0,1:T(2,128)(2,1)}), bf16[2,640,2048]{2,0,1:T(2,128)(2,1)}, u32[]{:S(2)}, u32[]{:S(2)}) async-start(bf16[2,640,2048]{2,0,1:T(2,128)(2,1)} %copy.49), calls=%async_computation.1 | async-start | bytes 10485760 | tf_op jit(solution)/shard_map/all_to_all | solution.py:48
  604.3 4.7 copy-start.1
Sparse Core Ops, SparseCore 0:
  346.8 79.0 reduce-scatter.1
where the time goes:
time: 635 us; the launch traced here: 627 us
  waiting for transfers between devices  408 us (64%)
  local copies, waits for them, and re-layouts  117 us (18%)
  matrix products  43.2 us (7%)
  other arithmetic  23 us (4%)
  starting transfers between devices  21.7 us (3%)
  between operations  14.5 us (2%)
    all_to_all x1, waiting for transfers between devices, body(): lax.all_to_all(send_rows, 'dp', split_axis=0, concat_axis=1, tiled=True)  109 us
    all_to_all x1, waiting for transfers between devices, body(): lax.all_to_all(result, 'dp', split_axis=1, concat_axis=0, tiled=True)  108 us
    all_to_all x1, waiting for transfers between devices, body(): lax.all_to_all(send_grads, 'dp', split_axis=0, concat_axis=1, tiled=True)  102 us
    all_to_all x1, waiting for transfers between devices, body(): lax.all_to_all(row_grads, 'dp', split_axis=1, concat_axis=0, tiled=True)  89.6 us
  transfers between devices with their start and end apart: 5, of which 4 were waited for; matrix products, arithmetic and copies ran while one was open for 15% of the time, Pallas kernels for 0%

commit v1 on v0

--- a/solution.py
+++ b/solution.py
@@ -2,6 +2,29 @@
 import jax.numpy as jnp
 from jax import lax
 from jax.sharding import PartitionSpec as P
+
+
+def split_up(shard, dim, size):
+    dims = shard.shape
+    blocks = shard.reshape(*dims[:dim], size, dims[dim] // size, *dims[dim + 1 :])
+    return jnp.moveaxis(blocks, dim, 0)
+
+
+def joined_along(tiles, dim):
+    tiles = jnp.moveaxis(tiles, 0, dim)
+    shape = tiles.shape
+    return tiles.reshape(*shape[:dim], shape[dim] * shape[dim + 1], *shape[dim + 2 :])
+
+
+def swapped_with_each(x, axis, split_dim, concat_dim):
+    size, position = (lax.axis_size(axis), lax.axis_index(axis))
+    parts = split_up(x, split_dim, size)
+    outs = [parts[position]]
+    for hop in range(1, size):
+        sent = parts[position ^ hop]
+        outs.append(lax.ppermute(sent, axis, [(i, i ^ hop) for i in range(size)]))
+    parts = jnp.stack(outs)[position ^ jnp.arange(size)]
+    return joined_along(parts, concat_dim)
 
 
 def expert_forward(arrived, w_gate, w_up, w_down):
@@ -45,9 +68,7 @@
     state = expert_forward(arrived, w_gate, w_up, w_down)
     arrived_grad = lax.all_to_all(send_grads, "dp", split_axis=0, concat_axis=1, tiled=True)
     gate_act, up_act, sigma_gate, smooth, hidden, result = state
-    returned = lax.all_to_all(result, "dp", split_axis=1, concat_axis=0, tiled=True).reshape(
-        slot_count, width
-    )
+    returned = swapped_with_each(result, "dp", 1, 0).reshape(slot_count, width)
     picked = returned[slot_index].reshape(tok_rows, top_k, width)
     layer_out = jnp.einsum("tk,tkd->td", gates, picked, preferred_element_type=jnp.float32).astype(
         jnp.bfloat16

time: 635 us -> 647 us (1.019)
  starting transfers between devices: 21.7 us -> 34.4 us
    ppermute x0 -> x7, waiting for transfers between devices: none -> 202 us  [swapped_with_each(): outs.append(lax.ppermute(sent, axis, [(i, i ^ hop) for i in range(size)]))]
    all_to_all x1 -> x0, waiting for transfers between devices: 108 us -> none  [body(): lax.all_to_all(result, 'dp', split_axis=1, concat_axis=0, tiled=True)]
    all_to_all x1, waiting for transfers between devices: 89.6 us -> 0.01 us  [body(): lax.all_to_all(row_grads, 'dp', split_axis=1, concat_axis=0, tiled=True)]
    ppermute x0 -> x7, starting transfers between devices: none -> 16.9 us  [swapped_with_each(): outs.append(lax.ppermute(sent, axis, [(i, i ^ hop) for i in range(size)]))]
    convert_element_type x1 -> x0, local copies, waits for them, and re-layouts: 11 us -> none  [expert_forward(): jnp.einsum('erf,efd->erd', hidden, w_down, preferred_element_type=jnp.flo...]
    all_to_all x1 -> x0, local copies, waits for them, and re-layouts: 7.26 us -> none  [body(): lax.all_to_all(result, 'dp', split_axis=1, concat_axis=0, tiled=True)]
  transfers between devices with their start and end apart: 5 -> 11, of which waited for: 4 -> 6; matrix products, arithmetic and copies ran while one was open for 15% -> 16% of each run, Pallas kernels for 0% -> 0%
where the time goes in v1:
time: 647 us; the launch traced here: 639 us
  waiting for transfers between devices  412 us (64%)
  local copies, waits for them, and re-layouts  113 us (17%)
  matrix products  38.9 us (6%)
  starting transfers between devices  34.4 us (5%)
  other arithmetic  25.8 us (4%)
  between operations  14.9 us (2%)
    ppermute x7, waiting for transfers between devices, swapped_with_each(): outs.append(lax.ppermute(sent, axis, [(i, i ^ hop) for i in range(size)]))  202 us
    all_to_all x1, waiting for transfers between devices, body(): lax.all_to_all(send_rows, 'dp', split_axis=0, concat_axis=1, tiled=True)  109 us
    all_to_all x1, waiting for transfers between devices, body(): lax.all_to_all(send_grads, 'dp', split_axis=0, concat_axis=1, tiled=True)  102 us
    ppermute x7, starting transfers between devices, swapped_with_each(): outs.append(lax.ppermute(sent, axis, [(i, i ^ hop) for i in range(size)]))  16.9 us
  transfers between devices with their start and end apart: 11, of which 6 were waited for; matrix products, arithmetic and copies ran while one was open for 16% of the time, Pallas kernels for 0%

profile of v1, /device:TPU:0, one launch (start us, length us, event | category | flops | bytes accessed | tf_op | source)
XLA Modules:
  0.0 639.4 jit_solution(18236620615264776908)
XLA Ops:
  9.3 4.5 reduce-window.6
  14.3 4.3 scatter_custom_fusion
  19.5 4.3 scatter_custom_fusion.1
  25.8 11.9 %gather_fusion.3 = bf16[1280,2048]{1,0:T(8,128)(2,1)} fusion(bf16[129,2048]{1,0:T(8,128)(2,1)} %concatenate.14, s32[2048]{0:T(1024)S(1)} %pad_clamp_fusion), kind=kCustom, calls=%fused_computation.3 | custom fusion | bytes 10490880 | tf_op jit(solution)/shard_map/gather | solution.py:65
  37.8 5.8 fusion
  43.5 7.3 %all-to-all-start.1 = ((bf16[16,80,2048]{2,1,0:T(8,128)(2,1)}), bf16[16,80,2048]{2,1,0:T(8,128)(2,1)}, u32[]{:S(2)}, u32[]{:S(2)}) async-start(bf16[16,80,2048]{2,1,0:T(8,128)(2,1)} %fusion), calls=%async_computation.1 | async-start | bytes 10485760 | tf_op jit(solution)/shard_map/all_to_all | solution.py:69
  52.7 11.9 %gather_fusion = bf16[1280,2048]{1,0:T(8,128)(2,1)} fusion(bf16[129,2048]{1,0:T(8,128)(2,1)} %concatenate.13, s32[2048]{0:T(1024)S(1)} %pad_clamp_fusion), kind=kCustom, calls=%fused_computation | custom fusion | bytes 10490880 | tf_op jit(solution)/shard_map/gather | solution.py:64
  64.7 101.9 %all-to-all-done.1 = bf16[16,80,2048]{2,1,0:T(8,128)(2,1)} async-done(((bf16[16,80,2048]{2,1,0:T(8,128)(2,1)}), bf16[16,80,2048]{2,1,0:T(8,128)(2,1)}, u32[]{:S(2)}, u32[]{:S(2)}) %all-to-all-start.1) | async-done | bytes 5242912 | tf_op jit(solution)/shard_map/all_to_all | solution.py:69
  166.6 4.7 all-to-all-start
  171.8 5.7 copy.48
  177.5 108.6 %all-to-all-done = bf16[16,80,2048]{2,1,0:T(8,128)(2,1)} async-done(((bf16[16,80,2048]{2,1,0:T(8,128)(2,1)}), bf16[16,80,2048]{2,1,0:T(8,128)(2,1)}, u32[]{:S(2)}, u32[]{:S(2)}) %all-to-all-start) | async-done | bytes 5242912 | tf_op jit(solution)/shard_map/all_to_all | solution.py:67
  292.5 4.1 fusion.21
  296.7 4.9 multiply_convert_fusion
  304.7 5.3 convert_bitcast_fusion
  309.9 8.6 %pad_maximum_fusion = bf16[2048,2,1152]{0,2,1:T(8,128)(2,1)} fusion(bf16[2048,2,384]{0,2,1:T(8,128)(2,1)S(1)} %fusion.3, bf16[2048,2,768]{0,2,1:T(8,128)(2,1)S(1)} %convert_bitcast_fusion), kind=kLoop, calls=%fused_computation.10 | loop fusion | flops 18874368 | bytes 18874368 | tf_op jit(solution)/shard_map/concatenate | solution.py:98
  318.6 5.4 fusion.23
  324.0 5.5 add_convert_fusion
  329.5 11.4 %copy.51 = bf16[2,640,2048]{2,0,1:T(2,128)(2,1)} copy(bf16[2,640,2048]{2,1,0:T(8,128)(2,1)} %add_convert_fusion) | data formatting | bytes 10485760 | tf_op jit(solution)/shard_map/convert_element_type | solution.py:86
  340.9 5.0 all-to-all-start.2
  346.1 4.4 convolution_convert_fusion
  353.2 3.4 collective-permute-start.6
  362.7 40.4 %collective-permute-done = bf16[2,80,2048]{2,1,0:T(8,128)(2,1)S(1)} collective-permute-done((bf16[2,80,2048]{2,1,0:T(8,128)(2,1)S(1)}, bf16[2,80,2048]{2,1,0:T(8,128)(2,1)S(1)}, u32[]{:S(2)}, u32[]{:S(2)}) %collective-permute-start) | collective-permute-done | bytes 655392 | tf_op jit(solution)/shard_map/ppermute | solution.py:25
  406.3 82.2 %collective-permute-done.1 = bf16[2,80,2048]{2,1,0:T(8,128)(2,1)S(1)} collective-permute-done((bf16[2,80,2048]{2,1,0:T(8,128)(2,1)S(1)}, bf16[2,80,2048]{2,1,0:T(8,128)(2,1)S(1)}, u32[]{:S(2)}, u32[]{:S(2)}) %collective-permute-start.1) | collective-permute-done | bytes 655392 | tf_op jit(solution)/shard_map/ppermute | solution.py:25
  488.5 4.0 collective-permute-start.3
  493.3 9.2 %collective-permute-done.2 = bf16[2,80,2048]{2,1,0:T(8,128)(2,1)S(1)} collective-permute-done((bf16[2,80,2048]{2,1,0:T(8,128)(2,1)S(1)}, bf16[2,80,2048]{2,1,0:T(8,128)(2,1)S(1)}, u32[]{:S(2)}, u32[]{:S(2)}) %collective-permute-start.2) | collective-permute-done | bytes 655392 | tf_op jit(solution)/shard_map/ppermute | solution.py:25
  503.4 70.0 %collective-permute-done.3 = bf16[2,80,2048]{2,1,0:T(8,128)(2,1)S(1)} collective-permute-done((bf16[2,80,2048]{2,1,0:T(8,128)(2,1)S(1)}, bf16[2,80,2048]{2,1,0:T(8,128)(2,1)S(1)}, u32[]{:S(2)}, u32[]{:S(2)}) %collective-permute-start.3) | collective-permute-done | bytes 655392 | tf_op jit(solution)/shard_map/ppermute | solution.py:25
  577.1 5.7 gather_fusion.1
  582.7 12.0 %gather_fusion.2 = bf16[1024,2048]{1,0:T(8,128)(2,1)} fusion(bf16[1280,2048]{1,0:T(8,128)(2,1)} %bitcast.106, s32[1024]{0:T(1024)S(1)} %broadcast_clamp_fusion), kind=kCustom, calls=%fused_computation.2 | custom fusion | bytes 8392704 | tf_op jit(solution)/shard_map/gather | solution.py:72
  594.7 3.4 fusion.1
  599.2 7.2 %copy.52 = bf16[2,8,80,2048]{3,2,0,1:T(8,128)(2,1)} copy(bf16[2,8,80,2048]{3,0,2,1:T(2,128)(2,1)} %bitcast.33) | data formatting | bytes 10485760 | tf_op jit(solution)/shard_map/all_to_all | solution.py:87
  606.4 12.2 %gather_fusion.4 = bf16[1024,2048]{1,0:T(8,128)(2,1)} fusion(bf16[1280,2048]{1,0:T(8,128)(2,1)} %bitcast.107, s32[1024]{0:T(1024)S(1)} %broadcast_clamp_fusion), kind=kCustom, calls=%fused_computation.4 | custom fusion | bytes 8392704 | tf_op jit(solution)/shard_map/gather | solution.py:90
  618.6 5.9 bitcast_reduce_fusion
  (78 shorter events, 43.6 us)
Async XLA Ops:
  7.2 289.5 %copy-start = (bf16[2,384,2048]{2,1,0:T(8,128)(2,1)S(1)}, bf16[2,384,2048]{2,1,0:T(8,128)(2,1)}, u32[]{:S(2)}) copy-start(bf16[2,384,2048]{2,1,0:T(8,128)(2,1)} %param.13) | copy-start | bytes 9437188
  43.5 123.1 %all-to-all-start.1 = ((bf16[16,80,2048]{2,1,0:T(8,128)(2,1)}), bf16[16,80,2048]{2,1,0:T(8,128)(2,1)}, u32[]{:S(2)}, u32[]{:S(2)}) async-start(bf16[16,80,2048]{2,1,0:T(8,128)(2,1)} %fusion), calls=%async_computation.1 | async-start | bytes 10485760 | tf_op jit(solution)/shard_map/all_to_all | solution.py:69
  166.6 119.6 %all-to-all-start = ((bf16[16,80,2048]{2,1,0:T(8,128)(2,1)}), bf16[16,80,2048]{2,1,0:T(8,128)(2,1)}, u32[]{:S(2)}, u32[]{:S(2)}) async-start(bf16[16,80,2048]{2,1,0:T(8,128)(2,1)} %bitcast.108), calls=%async_computation | async-start | bytes 10485760 | tf_op jit(solution)/shard_map/all_to_all | solution.py:67
  171.3 453.2 %reduce-scatter.2.cloned.1.call-start = ((), (), s32[]{:S(2)}) async-start(), calls=%async_computation.4 | async-start | bytes 11796480 | tf_op jit(solution)/shard_map/reduce_scatter | solution.py:97
  286.2 3.4 copy-start.2
  289.6 2.9 copy-start.1
  289.6 7.1 %slice-start = ((s8[5242880]{0:T(1024)(128)(4,1)}), s8[4194304]{0:T(1024)(128)(4,1)S(1)}, s32[]{:S(2)}) async-start(s8[5242880]{0:T(1024)(128)(4,1)} %bitcast.110), calls=%async_computation.5 | async-start | bytes 8388608
  292.5 4.1 slice-start.1
  301.6 3.0 copy-start.8
  301.6 3.0 copy-start.4
  301.6 3.0 copy-start.5
  318.6 5.4 copy-start.3
  318.6 5.4 copy-start.6
  340.9 5.0 copy-start.7
  340.9 258.3 %all-to-all-start.2 = ((bf16[2,640,2048]{2,0,1:T(2,128)(2,1)}), bf16[2,640,2048]{2,0,1:T(2,128)(2,1)}, u32[]{:S(2)}, u32[]{:S(2)}) async-start(bf16[2,640,2048]{2,0,1:T(2,128)(2,1)} %copy.51), calls=%async_computation.2 | async-start | bytes 10485760 | tf_op jit(solution)/shard_map/all_to_all | solution.py:87
  351.1 52.0 %collective-permute-start = (bf16[2,80,2048]{2,1,0:T(8,128)(2,1)S(1)}, bf16[2,80,2048]{2,1,0:T(8,128)(2,1)S(1)}, u32[]{:S(2)}, u32[]{:S(2)}) collective-permute-start(bf16[2,80,2048]{2,1,0:T(8,128)(2,1)S(1)} %get-tuple-element.26), channel_id=1, source_target_pairs={{0,4},{4,0},{8,12},{12,8},{16,20},{20,16},{24,28},{28,24},{1,5},{5... | collective-permute-start | bytes 1966088 | tf_op jit(solution)/shard_map/ppermute | solution.py:25
  353.2 223.0 %collective-permute-start.6 = (bf16[2,80,2048]{2,1,0:T(8,128)(2,1)S(1)}, bf16[2,80,2048]{2,1,0:T(8,128)(2,1)S(1)}, u32[]{:S(2)}, u32[]{:S(2)}) collective-permute-start(bf16[2,80,2048]{2,1,0:T(8,128)(2,1)S(1)} %get-tuple-element.20), channel_id=1, source_target_pairs={{0,28},{4,24},{8,20},{12,16},{16,12},{20,8},{24,4},{28,0},{1,29},{... | collective-permute-start | bytes 1966088 | tf_op jit(solution)/shard_map/ppermute | solution.py:25
  356.5 218.7 %collective-permute-start.5 = (bf16[2,80,2048]{2,1,0:T(8,128)(2,1)S(1)}, bf16[2,80,2048]{2,1,0:T(8,128)(2,1)S(1)}, u32[]{:S(2)}, u32[]{:S(2)}) collective-permute-start(bf16[2,80,2048]{2,1,0:T(8,128)(2,1)S(1)} %get-tuple-element.21), channel_id=1, source_target_pairs={{0,24},{4,28},{8,16},{12,20},{16,8},{20,12},{24,0},{28,4},{1,25},{... | collective-permute-start | bytes 1966088 | tf_op jit(solution)/shard_map/ppermute | solution.py:25
  356.6 217.7 %collective-permute-start.4 = (bf16[2,80,2048]{2,1,0:T(8,128)(2,1)S(1)}, bf16[2,80,2048]{2,1,0:T(8,128)(2,1)S(1)}, u32[]{:S(2)}, u32[]{:S(2)}) collective-permute-start(bf16[2,80,2048]{2,1,0:T(8,128)(2,1)S(1)} %get-tuple-element.22), channel_id=1, source_target_pairs={{0,20},{4,16},{8,28},{12,24},{16,4},{20,0},{24,12},{28,8},{1,21},{... | collective-permute-start | bytes 1966088 | tf_op jit(solution)/shard_map/ppermute | solution.py:25
  358.5 129.9 %collective-permute-start.1 = (bf16[2,80,2048]{2,1,0:T(8,128)(2,1)S(1)}, bf16[2,80,2048]{2,1,0:T(8,128)(2,1)S(1)}, u32[]{:S(2)}, u32[]{:S(2)}) collective-permute-start(bf16[2,80,2048]{2,1,0:T(8,128)(2,1)S(1)} %get-tuple-element.25), channel_id=1, source_target_pairs={{0,8},{4,12},{8,0},{12,4},{16,24},{20,28},{24,16},{28,20},{1,9},{5... | collective-permute-start | bytes 1966088 | tf_op jit(solution)/shard_map/ppermute | solution.py:25
  403.2 99.3 %collective-permute-start.2 = (bf16[2,80,2048]{2,1,0:T(8,128)(2,1)S(1)}, bf16[2,80,2048]{2,1,0:T(8,128)(2,1)S(1)}, u32[]{:S(2)}, u32[]{:S(2)}) collective-permute-start(bf16[2,80,2048]{2,1,0:T(8,128)(2,1)S(1)} %get-tuple-element.24), channel_id=1, source_target_pairs={{0,12},{4,8},{8,4},{12,0},{16,28},{20,24},{24,20},{28,16},{1,13},{... | collective-permute-start | bytes 1966088 | tf_op jit(solution)/shard_map/ppermute | solution.py:25
  488.5 84.9 %collective-permute-start.3 = (bf16[2,80,2048]{2,1,0:T(8,128)(2,1)S(1)}, bf16[2,80,2048]{2,1,0:T(8,128)(2,1)S(1)}, u32[]{:S(2)}, u32[]{:S(2)}) collective-permute-start(bf16[2,80,2048]{2,1,0:T(8,128)(2,1)S(1)} %get-tuple-element.23), channel_id=1, source_target_pairs={{0,16},{4,20},{8,24},{12,28},{16,0},{20,4},{24,8},{28,12},{1,17},{... | collective-permute-start | bytes 1966088 | tf_op jit(solution)/shard_map/ppermute | solution.py:25
Sparse Core Ops, SparseCore 0:
  318.7 76.7 reduce-scatter.1
